TPU v7x, 256 devices: a whole 4x4x8 slice. The times are simulated.
256 devices in a mesh: bucket: 64 (over x, y, z_hi), span: 4 (over z_lo, core).
Axes of the slice: x: 4, y: 4, z: 8 (z_hi: 4, z_lo: 2; z = z_hi * 2 + z_lo), core: 2. Of those that a mesh axis runs over, the one named last changes fastest.
Arguments:
- source_table: float32 [65536, 400], P('bucket'), may hold values from -6 to 6
- target_table: float32 [65536, 400], P('bucket'), may hold values from -6 to 6
- source_state: float32 [65536], P('bucket'), may hold values from 0.001 to 0.03
- target_state: float32 [65536], P('bucket'), may hold values from 0.001 to 0.03
- relation: float32 [16, 400], replicated, may hold values from -3 to 3
- relation_state: float32 [16], replicated, may hold values from 10 to 1000
- plan: int32 [64], replicated, may hold values from 0 to 63, each once
- source_index: int32 [64, 10240], P('bucket', 'span'), may hold values from 0 to 1023
- target_index: int32 [64, 10240], P('bucket', 'span'), may hold values from 0 to 1023
- relation_index: int32 [64, 10240], P('bucket', 'span'), may hold values from 0 to 15
- edge_counts: int32 [64], P('bucket'), may hold values from 1280 to 10240, as said below
Outputs:
- new_source: float32 [65536, 400], P('bucket')
- new_target: float32 [65536, 400], P('bucket')
- new_relation: float32 [16, 400], replicated
Inputs may be any that keep to these rules, and one draw needn't show every extreme that they name: `plan`: each partition index appears once. `edge_counts`: one bucket has exactly 10240 live slots and another exactly 1280.
All inputs are finite; a program needn't handle non-finite values.
Results may differ from a plain program's by a relative error of at most 0.0028.
The roundings to bfloat16 on the way count: a program that leaves them out, or rounds other values in their place, can miss the bound.
Values may be sent and summed in bfloat16 or wider, within the bound.
A program may use at most 64 MiB of HBM per device.

v0:
```python
import jax
import jax.numpy as jnp
from jax import lax
from jax.sharding import PartitionSpec as P

E_CH = 640
LEARN_RATE = 0.25
NEG_WEIGHT = 0.03125


def span_terms(head_rows, relation_rows, tail_rows, live_mask):
    half_width = head_rows.shape[1] // 2
    head_float = head_rows.astype(jnp.float32)
    head_real = head_float[:, :half_width]
    head_imag = head_float[:, half_width:]
    rel_real = relation_rows[:, :half_width]
    rel_imag = relation_rows[:, half_width:]
    query_rows = jnp.concatenate(
        [head_real * rel_real - head_imag * rel_imag, head_real * rel_imag + head_imag * rel_real],
        axis=1,
    ).astype(jnp.bfloat16)
    scores = lax.dot_general(
        query_rows, tail_rows, (((1,), (1,)), ((), ())), preferred_element_type=jnp.float32
    )
    diagonal = lax.broadcasted_iota(jnp.int32, scores.shape, 0) == lax.broadcasted_iota(
        jnp.int32, scores.shape, 1
    )
    weights = jnp.where(diagonal, -jax.nn.sigmoid(-scores), NEG_WEIGHT * jax.nn.sigmoid(scores))
    coefficients = (weights * live_mask[:, None] * live_mask[None, :]).astype(jnp.bfloat16)
    grad_query = jnp.dot(coefficients, tail_rows, preferred_element_type=jnp.float32)
    grad_tail = lax.dot_general(
        coefficients, query_rows, (((0,), (0,)), ((), ())), preferred_element_type=jnp.float32
    )
    query_real = grad_query[:, :half_width]
    query_imag = grad_query[:, half_width:]
    grad_head = jnp.concatenate(
        [
            query_real * rel_real + query_imag * rel_imag,
            query_imag * rel_real - query_real * rel_imag,
        ],
        axis=1,
    )
    grad_relation = jnp.concatenate(
        [
            query_real * head_real + query_imag * head_imag,
            query_imag * head_real - query_real * head_imag,
        ],
        axis=1,
    )
    return (grad_head, grad_relation, grad_tail)


def row_adagrad(weights, accumulated, gradient):
    summed = accumulated + jnp.mean(gradient * gradient, axis=1)
    return weights - LEARN_RATE * gradient / jnp.sqrt(summed)[:, None]


def route_blocks(row_block, selector):
    buckets = lax.axis_size("bucket")
    rows_total, feature_width = row_block.shape
    pieces = row_block.reshape(buckets, rows_total // buckets, feature_width)
    spread_out = lax.all_to_all(pieces, "bucket", split_axis=0, concat_axis=0, tiled=True)
    picker = (selector[:, None] == jnp.arange(buckets, dtype=jnp.int32)[None, :]).astype(
        jnp.float32
    )
    chosen = jnp.einsum("ij,jrd->ird", picker, spread_out, precision=lax.Precision.HIGHEST)
    arrived = lax.all_to_all(chosen, "bucket", split_axis=0, concat_axis=0, tiled=True)
    return arrived.reshape(rows_total, feature_width)


def per_device(
    source_table,
    target_table,
    source_state,
    target_state,
    relation,
    relation_state,
    plan,
    source_index,
    target_index,
    relation_index,
    edge_counts,
):
    num_buckets = lax.axis_size("bucket")
    lane_index = lax.axis_index("span")
    inverse = jnp.zeros_like(plan).at[plan].set(jnp.arange(num_buckets, dtype=jnp.int32))
    live_limit = edge_counts[0]
    table_rows, feature_width = source_table.shape
    spans_here = source_index.shape[1] // E_CH
    relation_count = relation.shape[0]
    relation_iota = jnp.arange(relation_count, dtype=jnp.int32)
    row_iota = jnp.arange(table_rows, dtype=jnp.int32)
    head_table = source_index.reshape(spans_here, E_CH)
    tail_table = target_index.reshape(spans_here, E_CH)
    kind_table = relation_index.reshape(spans_here, E_CH)
    starts = (lane_index * spans_here + jnp.arange(spans_here, dtype=jnp.int32)) * E_CH
    source_low = source_table.astype(jnp.bfloat16)
    target_low = route_blocks(target_table, plan).astype(jnp.bfloat16)

    def add_span(position_now, carried):
        span_start = starts[position_now]

        def compute(values):
            source_grad, target_grad, rel_grad = values
            slots = span_start + jnp.arange(E_CH, dtype=jnp.int32)
            live_mask = (slots < live_limit).astype(jnp.float32)
            head_ids = lax.dynamic_index_in_dim(head_table, position_now, 0, keepdims=False)
            tail_ids = lax.dynamic_index_in_dim(tail_table, position_now, 0, keepdims=False)
            kind_ids = lax.dynamic_index_in_dim(kind_table, position_now, 0, keepdims=False)
            one_hot = (kind_ids[:, None] == relation_iota[None, :]).astype(jnp.float32)
            relation_rows = jnp.dot(one_hot, relation, precision=lax.Precision.HIGHEST)
            head_match = head_ids[:, None] == row_iota[None, :]
            tail_match = tail_ids[:, None] == row_iota[None, :]
            head_rows = jnp.dot(
                head_match.astype(jnp.bfloat16), source_low, preferred_element_type=jnp.float32
            ).astype(jnp.bfloat16)
            tail_rows = jnp.dot(
                tail_match.astype(jnp.bfloat16), target_low, preferred_element_type=jnp.float32
            ).astype(jnp.bfloat16)
            grad_head, grad_relation, grad_tail = span_terms(
                head_rows, relation_rows, tail_rows, live_mask
            )
            rel_add = lax.dot_general(
                one_hot, grad_relation, (((0,), (0,)), ((), ())), precision=lax.Precision.HIGHEST
            )
            head_add = lax.dot_general(
                head_match.astype(jnp.float32),
                grad_head,
                (((0,), (0,)), ((), ())),
                precision=lax.Precision.HIGHEST,
            )
            tail_add = lax.dot_general(
                tail_match.astype(jnp.float32),
                grad_tail,
                (((0,), (0,)), ((), ())),
                precision=lax.Precision.HIGHEST,
            )
            return (source_grad + head_add, target_grad + tail_add, rel_grad + rel_add)

        def keep_values(values):
            return values

        return lax.cond(span_start < live_limit, compute, keep_values, carried)

    start_values = (
        jnp.zeros((table_rows, feature_width), jnp.float32),
        jnp.zeros((table_rows, feature_width), jnp.float32),
        jnp.zeros((relation_count, feature_width), jnp.float32),
    )
    source_grad, target_grad, rel_grad = lax.fori_loop(0, spans_here, add_span, start_values)
    rel_total = lax.psum(rel_grad, ("bucket", "span"))
    new_relation = row_adagrad(relation, relation_state, rel_total)
    source_sum, target_sum = lax.psum((source_grad, target_grad), "span")
    target_home = route_blocks(target_sum, inverse)
    new_source = row_adagrad(source_table, source_state, source_sum)
    new_target = row_adagrad(target_table, target_state, target_home)
    return (new_source, new_target, new_relation)


def solution(mesh):
    placed = (
        P("bucket", None),
        P("bucket", None),
        P("bucket"),
        P("bucket"),
        P(),
        P(),
        P(),
        P("bucket", "span"),
        P("bucket", "span"),
        P("bucket", "span"),
        P("bucket"),
    )
    return jax.shard_map(
        per_device,
        mesh=mesh,
        in_specs=placed,
        out_specs=(P("bucket", None), P("bucket", None), P()),
        check_vma=False,
    )
```

profile of v0, /device:TPU:1, one launch (start us, length us, event | category | flops | bytes accessed | tf_op | source)
XLA Modules:
  0.0 449.8 jit_solution(263234524063115752)
XLA Ops:
  7.2 1.8 copy.25
  9.0 66.5 %all_to_all.20 = f32[64,16,400]{2,1,0:T(8,128)S(1)} all-to-all(f32[64,16,400]{2,1,0:T(8,128)S(1)} %bitcast.26), channel_id=1, replica_groups=mesh['bucket'=64,'span'=4] {'bucket'}, dimensions={0} | all-to-all | bytes 3276800 | tf_op jit(solution)/shard_map/all_to_all | solution.py:62
  75.5 2.5 fusion.57
  78.0 1.5 copy.27
  79.6 6.5 %all-to-all-start.1 = ((bf16[64,16,400]{2,1,0:T(8,128)(2,1)}), bf16[64,16,400]{2,1,0:T(8,128)(2,1)S(1)}, u32[]{:S(2)}, u32[]{:S(2)}) async-start(bf16[64,16,400]{2,1,0:T(8,128)(2,1)} %copy.27), calls=%async_computation.1 | async-start | bytes 2097152 | tf_op jit(solution)/shard_map/all_to_all | solution.py:67
  86.5 1.4 copy.24
  87.9 21.9 %all-to-all-done.1 = bf16[64,16,400]{2,1,0:T(8,128)(2,1)S(1)} async-done(((bf16[64,16,400]{2,1,0:T(8,128)(2,1)}), bf16[64,16,400]{2,1,0:T(8,128)(2,1)S(1)}, u32[]{:S(2)}, u32[]{:S(2)}) %all-to-all-start.1) | async-done | bytes 819232 | tf_op jit(solution)/shard_map/all_to_all | solution.py:67
  109.7 1.0 copy-done.7
  111.5 63.1 %while.19 = (s32[]{:T(128)}, f32[1024,400]{0,1:T(8,128)S(1)}, f32[1024,400]{0,1:T(8,128)S(1)}, f32[16,400]{1,0:T(8,128)S(1)}, s32[4]{0:T(128)S(1)}, /*index=5*/s...) while((s32[]{:T(128)}, f32[1024,400]{0,1:T(8,128)S(1)}, ...), condition=%wide.region_3.4_spmd.clone.clone, body=%wide.region_0.3_spmd.clone.clone.sunk | while | flops 8435658752 | bytes 31468124 | solution.py:150
  113.3 13.9 %conditional.4 = ((f32[1024,400]{0,1:T(8,128)S(1)}, f32[1024,400]{0,1:T(8,128)S(1)}, f32[16,400]{1,0:T(8,128)S(1)})) conditional(s32[]{:T(128)} %convert_element_type.60, (f32[1024,400]{0,1:T(8,128)S(1)}, f32[1024,400]{0,1:T(8,128)S(1)}, f32[16,400]{1,0:T(8,128)S(1)}) %tuple.60, (s32[]{:T(128)}, s32[4,640]{1,0:T(4,128)S(1)}, s32[1024]{0:T(1024)S(1)}, ...), branch_computations={%region_1.1_spmd, %region_2.0_spmd} | conditional | flops 8435658752 | bytes 31463662 | solution.py:143
  113.4 2.3 fusion.32
  115.7 0.9 fusion.29
  116.7 1.3 fusion.49
  117.9 0.7 fusion.41
  118.8 0.9 multiply_convert_fusion
  120.4 0.7 fusion.67
  121.3 0.7 convolution_add_fusion
  122.1 2.6 fusion.15
  124.7 2.6 fusion.12
  129.1 13.9 %conditional.4 = ((f32[1024,400]{0,1:T(8,128)S(1)}, f32[1024,400]{0,1:T(8,128)S(1)}, f32[16,400]{1,0:T(8,128)S(1)})) conditional(s32[]{:T(128)} %convert_element_type.60, (f32[1024,400]{0,1:T(8,128)S(1)}, f32[1024,400]{0,1:T(8,128)S(1)}, f32[16,400]{1,0:T(8,128)S(1)}) %tuple.60, (s32[]{:T(128)}, s32[4,640]{1,0:T(4,128)S(1)}, s32[1024]{0:T(1024)S(1)}, ...), branch_computations={%region_1.1_spmd, %region_2.0_spmd} | conditional | flops 8435658752 | bytes 31463662 | solution.py:143
  129.2 2.3 fusion.32
  131.5 0.9 fusion.29
  132.4 1.3 fusion.49
  133.7 0.7 fusion.41
  134.6 0.9 multiply_convert_fusion
  135.5 0.7 fusion.43
  136.2 0.7 fusion.67
  137.1 0.7 convolution_add_fusion
  137.8 2.6 fusion.15
  140.4 2.6 fusion.12
  144.9 13.9 %conditional.4 = ((f32[1024,400]{0,1:T(8,128)S(1)}, f32[1024,400]{0,1:T(8,128)S(1)}, f32[16,400]{1,0:T(8,128)S(1)})) conditional(s32[]{:T(128)} %convert_element_type.60, (f32[1024,400]{0,1:T(8,128)S(1)}, f32[1024,400]{0,1:T(8,128)S(1)}, f32[16,400]{1,0:T(8,128)S(1)}) %tuple.60, (s32[]{:T(128)}, s32[4,640]{1,0:T(4,128)S(1)}, s32[1024]{0:T(1024)S(1)}, ...), branch_computations={%region_1.1_spmd, %region_2.0_spmd} | conditional | flops 8435658752 | bytes 31463662 | solution.py:143
  145.0 2.3 fusion.32
  147.3 0.9 fusion.29
  148.2 1.3 fusion.49
  149.5 0.7 fusion.41
  150.4 0.9 multiply_convert_fusion
  152.0 0.7 fusion.67
  152.9 0.7 convolution_add_fusion
  153.6 2.6 fusion.15
  156.2 2.6 fusion.12
  160.7 13.9 %conditional.4 = ((f32[1024,400]{0,1:T(8,128)S(1)}, f32[1024,400]{0,1:T(8,128)S(1)}, f32[16,400]{1,0:T(8,128)S(1)})) conditional(s32[]{:T(128)} %convert_element_type.60, (f32[1024,400]{0,1:T(8,128)S(1)}, f32[1024,400]{0,1:T(8,128)S(1)}, f32[16,400]{1,0:T(8,128)S(1)}) %tuple.60, (s32[]{:T(128)}, s32[4,640]{1,0:T(4,128)S(1)}, s32[1024]{0:T(1024)S(1)}, ...), branch_computations={%region_1.1_spmd, %region_2.0_spmd} | conditional | flops 8435658752 | bytes 31463662 | solution.py:143
  160.7 2.3 fusion.32
  163.0 0.9 fusion.29
  164.0 1.3 fusion.49
  165.3 0.7 fusion.41
  166.1 0.9 multiply_convert_fusion
  167.7 0.7 fusion.67
  168.7 0.7 convolution_add_fusion
  169.4 2.6 fusion.15
  172.0 2.6 fusion.12
  174.6 1.9 copy.28
  176.5 91.2 %all-reduce.3.cloned.1.call-done = (f32[1024,400]{0,1:T(8,128)}, f32[64,16,400]{2,1,0:T(8,128)}) async-done(((f32[1024,400]{0,1:T(8,128)}, f32[64,16,400]{2,1,0:T(8,128)}), (f32[1024,400]{0,1:T(8,128)}, f32[64,16,400]{2,1,0:T(8,128)})) %all-reduce.3.cloned.1.call-update) | async-done | bytes 3276816 | tf_op jit(solution)/shard_map/psum | solution.py:153
  267.6 11.7 %all-to-all-start.2 = ((f32[64,16,400]{2,1,0:T(8,128)}), f32[64,16,400]{2,1,0:T(8,128)S(1)}, u32[]{:S(2)}, u32[]{:S(2)}) async-start(f32[64,16,400]{2,1,0:T(8,128)} %get-tuple-element.395), calls=%async_computation.2 | async-start | bytes 4194304 | tf_op jit(solution)/shard_map/all_to_all | solution.py:62
  279.4 1.0 scatter_custom_fusion
  280.4 42.4 %all-to-all-done.2 = f32[64,16,400]{2,1,0:T(8,128)S(1)} async-done(((f32[64,16,400]{2,1,0:T(8,128)}), f32[64,16,400]{2,1,0:T(8,128)S(1)}, u32[]{:S(2)}, u32[]{:S(2)}) %all-to-all-start.2) | async-done | bytes 1638432 | tf_op jit(solution)/shard_map/all_to_all | solution.py:62
  322.8 2.5 fusion.55
  325.3 2.5 copy.30
  327.8 8.5 %all-to-all-start.3 = ((f32[64,16,400]{2,1,0:T(8,128)}), f32[64,16,400]{2,1,0:T(8,128)}, u32[]{:S(2)}, u32[]{:S(2)}) async-start(f32[64,16,400]{2,1,0:T(8,128)} %copy.30), calls=%async_computation.3 | async-start | bytes 4194304 | tf_op jit(solution)/shard_map/all_to_all | solution.py:67
  336.3 94.5 %psum.23 = f32[16,400]{1,0:T(8,128)S(1)} all-reduce(f32[16,400]{1,0:T(8,128)S(1)} %get-tuple-element.298), channel_id=1, replica_groups=mesh['bucket'=64,'span'=4] {'bucket','span'}, use_global_device_ids=true, to_apply=%region_9.10 | all-reduce | flops 6400 | bytes 51200 | tf_op jit(solution)/shard_map/psum | solution.py:151
  431.0 0.7 divide_subtract_fusion.1
  431.8 1.6 divide_subtract_fusion
  433.5 3.3 multiply_reduce_fusion
  437.0 3.2 fusion.54
  440.2 2.7 copy.34
  (92 shorter events, 7.7 us)
Async XLA Ops:
  9.0 66.5 %copy-start.1 = (f32[1024,400]{1,0:T(8,128)}, f32[1024,400]{1,0:T(8,128)S(1)}, u32[]{:S(2)}) copy-start(f32[1024,400]{1,0:T(8,128)S(1)} %copy.25) | copy-start | bytes 4915204
  9.0 66.5 %copy-start.14 = (s32[64]{0:T(128)S(1)}, s32[64]{0:T(128)}, u32[]{:S(2)}) copy-start(s32[64]{0:T(128)} %param.21) | copy-start | bytes 772
  78.0 8.3 %copy-start.9 = (s32[1,2560]{1,0:T(1,128)S(1)}, s32[1,2560]{1,0:T(1,128)}, u32[]{:S(2)}) copy-start(s32[1,2560]{1,0:T(1,128)} %param.22) | copy-start | bytes 30724
  78.0 8.4 %copy-start.10 = (s32[1,2560]{1,0:T(1,128)S(1)}, s32[1,2560]{1,0:T(1,128)}, u32[]{:S(2)}) copy-start(s32[1,2560]{1,0:T(1,128)} %param.23) | copy-start | bytes 30724
  78.0 8.4 %copy-start.11 = (s32[1,2560]{1,0:T(1,128)S(1)}, s32[1,2560]{1,0:T(1,128)}, u32[]{:S(2)}) copy-start(s32[1,2560]{1,0:T(1,128)} %param.24) | copy-start | bytes 30724
  79.6 6.9 %copy-start.4 = (f32[1024,400]{0,1:T(8,128)S(1)}, f32[1024,400]{0,1:T(8,128)}, u32[]{:S(2)}) copy-start(f32[1024,400]{0,1:T(8,128)} %param.15) | copy-start | bytes 4915204
  79.6 30.1 %all-to-all-start.1 = ((bf16[64,16,400]{2,1,0:T(8,128)(2,1)}), bf16[64,16,400]{2,1,0:T(8,128)(2,1)S(1)}, u32[]{:S(2)}, u32[]{:S(2)}) async-start(bf16[64,16,400]{2,1,0:T(8,128)(2,1)} %copy.27), calls=%async_computation.1 | async-start | bytes 2097152 | tf_op jit(solution)/shard_map/all_to_all | solution.py:67
  86.1 181.6 %all-reduce.3.cloned.1.call-start = ((), (), s32[]{:S(2)}) async-start(), calls=%async_computation.4 | async-start | bytes 7471104 | tf_op jit(solution)/shard_map/psum | solution.py:153
  109.7 1.0 copy-start.7
  110.7 0.8 copy-start.6
  113.4 2.3 copy-start.8
  129.2 2.3 copy-start.8
  144.9 2.3 copy-start.8
  160.7 2.3 copy-start.8
  174.5 1.9 copy-start
  267.6 55.2 %all-to-all-start.2 = ((f32[64,16,400]{2,1,0:T(8,128)}), f32[64,16,400]{2,1,0:T(8,128)S(1)}, u32[]{:S(2)}, u32[]{:S(2)}) async-start(f32[64,16,400]{2,1,0:T(8,128)} %get-tuple-element.395), calls=%async_computation.2 | async-start | bytes 4194304 | tf_op jit(solution)/shard_map/all_to_all | solution.py:62
  327.8 103.1 %copy-start.15 = (f32[16]{0:T(128)S(1)}, f32[16]{0:T(128)}, u32[]{:S(2)}) copy-start(f32[16]{0:T(128)} %param.20) | copy-start | bytes 196
  327.8 103.8 %copy-start.3 = (f32[1024,400]{0,1:T(8,128)S(1)}, f32[1024,400]{0,1:T(8,128)}, u32[]{:S(2)}) copy-start(f32[1024,400]{0,1:T(8,128)} %get-tuple-element.394) | copy-start | bytes 4915204
  327.8 105.7 %all-to-all-start.3 = ((f32[64,16,400]{2,1,0:T(8,128)}), f32[64,16,400]{2,1,0:T(8,128)}, u32[]{:S(2)}, u32[]{:S(2)}) async-start(f32[64,16,400]{2,1,0:T(8,128)} %copy.30), calls=%async_computation.3 | async-start | bytes 4194304 | tf_op jit(solution)/shard_map/all_to_all | solution.py:67
  336.3 95.5 %copy-start.12 = (f32[1024]{0:T(1024)S(1)}, f32[1024]{0:T(1024)}, u32[]{:S(2)}) copy-start(f32[1024]{0:T(1024)} %param.17) | copy-start | bytes 12292
  336.3 95.5 %copy-start.5 = (f32[1024,400]{0,1:T(8,128)S(1)}, f32[1024,400]{0,1:T(8,128)}, u32[]{:S(2)}) copy-start(f32[1024,400]{0,1:T(8,128)} %param.15) | copy-start | bytes 4915204
  433.5 3.5 copy-start.13
  433.5 3.5 copy-start.2
Sparse Core Ops, SparseCore 0:
  176.6 90.9 all-reduce.2
where the time goes:
time: 451 us; the launch traced here: 450 us
  blocking collectives  161 us (36%)
  waiting for transfers between devices  155 us (34%)
  matrix products  53.2 us (12%)
  starting transfers between devices  26.9 us (6%)
  local copies, waits for them, and re-layouts  17.6 us (4%)
  other arithmetic  15.7 us (3%)
  between operations  14.3 us (3%)
  loops' own time  5.71 us (1%)
    psum x1, blocking collectives, per_device(): rel_total = lax.psum(rel_grad, ('bucket', 'span'))  94.5 us
    psum x1, waiting for transfers between devices, per_device(): source_sum, target_sum = lax.psum((source_grad, target_grad), 'span')  91.2 us
    all_to_all x1, blocking collectives, route_blocks(): lax.all_to_all(pieces, 'bucket', split_axis=0, concat_axis=0, tiled=True)  66.5 us
    all_to_all x1, waiting for transfers between devices, route_blocks(): lax.all_to_all(pieces, 'bucket', split_axis=0, concat_axis=0, tiled=True)  42.4 us
    all_to_all x2, waiting for transfers between devices, route_blocks(): lax.all_to_all(chosen, 'bucket', split_axis=0, concat_axis=0, tiled=True)  21.9 us
    all_to_all x2, starting transfers between devices, route_blocks(): lax.all_to_all(chosen, 'bucket', split_axis=0, concat_axis=0, tiled=True)  15 us
    all_to_all x1, starting transfers between devices, route_blocks(): lax.all_to_all(pieces, 'bucket', split_axis=0, concat_axis=0, tiled=True)  11.7 us
    dot_general x4, matrix products, compute(): lax.dot_general(tail_match.astype(jnp.float32), grad_tail, (((0,), (0,)),...  10.3 us
  transfers between devices with their start and end apart: 4, of which 3 were waited for; matrix products, arithmetic and copies ran while one was open for 1% of the time, Pallas kernels for 0%

commit v1 on v0

--- a/solution.py
+++ b/solution.py
@@ -148,7 +148,7 @@
         jnp.zeros((relation_count, feature_width), jnp.float32),
     )
     source_grad, target_grad, rel_grad = lax.fori_loop(0, spans_here, add_span, start_values)
-    rel_total = lax.psum(rel_grad, ("bucket", "span"))
+    rel_total = jnp.sum(lax.all_gather(rel_grad, ("bucket", "span")), axis=0)
     new_relation = row_adagrad(relation, relation_state, rel_total)
     source_sum, target_sum = lax.psum((source_grad, target_grad), "span")
     target_home = route_blocks(target_sum, inverse)

time: 451 us -> 427 us (0.947)
  the two profiles are of different devices: /device:TPU:1 before, /device:TPU:32 now
where the time goes in v1:
time: 427 us; the launch traced here: 426 us
  waiting for transfers between devices  262 us (61%)
  blocking collectives  66.7 us (16%)
  starting transfers between devices  26.9 us (6%)
  local copies, waits for them, and re-layouts  18.6 us (4%)
  matrix products  17 us (4%)
  between operations  15.8 us (4%)
  other arithmetic  14.5 us (3%)
  loops' own time  5.16 us (1%)
    psum x1, waiting for transfers between devices, per_device(): source_sum, target_sum = lax.psum((source_grad, target_grad), 'span')  123 us
    all_to_all x2, waiting for transfers between devices, route_blocks(): lax.all_to_all(chosen, 'bucket', split_axis=0, concat_axis=0, tiled=True)  75.5 us
    all_to_all x1, blocking collectives, route_blocks(): lax.all_to_all(pieces, 'bucket', split_axis=0, concat_axis=0, tiled=True)  66.7 us
    all_to_all x1, waiting for transfers between devices, route_blocks(): lax.all_to_all(pieces, 'bucket', split_axis=0, concat_axis=0, tiled=True)  63 us
    all_to_all x2, starting transfers between devices, route_blocks(): lax.all_to_all(chosen, 'bucket', split_axis=0, concat_axis=0, tiled=True)  13.4 us
    all_to_all x1, starting transfers between devices, route_blocks(): lax.all_to_all(pieces, 'bucket', split_axis=0, concat_axis=0, tiled=True)  13.3 us
    unnamed x36, local copies, waits for them, and re-layouts  8.66 us
  transfers between devices with their start and end apart: 5, of which 4 were waited for; matrix products, arithmetic and copies ran while one was open for 4% of the time, Pallas kernels for 0%

profile of v1, /device:TPU:32, one launch (start us, length us, event | category | flops | bytes accessed | tf_op | source)
XLA Modules:
  0.0 426.4 jit_solution(15642644637662864471)
XLA Ops:
  8.0 1.8 copy.25
  9.9 0.0 copy-start.15
  9.9 66.7 %all_to_all.20 = f32[64,16,400]{2,1,0:T(8,128)S(1)} all-to-all(f32[64,16,400]{2,1,0:T(8,128)S(1)} %bitcast.27), channel_id=1, replica_groups=mesh['bucket'=64,'span'=4] {'bucket'}, dimensions={0} | all-to-all | bytes 3276800 | tf_op jit(solution)/shard_map/all_to_all | solution.py:62
  76.6 2.5 fusion.57
  79.1 0.0 copy-start.10
  79.1 0.0 copy-start.11
  79.1 0.0 copy-start.12
  79.1 1.5 copy.27
  80.7 6.6 %all-to-all-start.1 = ((bf16[64,16,400]{2,1,0:T(8,128)(2,1)}), bf16[64,16,400]{2,1,0:T(8,128)(2,1)S(1)}, u32[]{:S(2)}, u32[]{:S(2)}) async-start(bf16[64,16,400]{2,1,0:T(8,128)(2,1)} %copy.27), calls=%async_computation.1 | async-start | bytes 2097152 | tf_op jit(solution)/shard_map/all_to_all | solution.py:67
  87.3 0.2 all-reduce.3.cloned.1.call-start
  87.7 1.4 copy.24
  89.1 28.5 %all-to-all-done.1 = bf16[64,16,400]{2,1,0:T(8,128)(2,1)S(1)} async-done(((bf16[64,16,400]{2,1,0:T(8,128)(2,1)}), bf16[64,16,400]{2,1,0:T(8,128)(2,1)S(1)}, u32[]{:S(2)}, u32[]{:S(2)}) %all-to-all-start.1) | async-done | bytes 819232 | tf_op jit(solution)/shard_map/all_to_all | solution.py:67
  117.6 1.0 copy-done.8
  118.5 0.2 broadcast.58.clone
  118.7 0.2 broadcast.58
  118.9 0.4 copy-done.7
  119.3 21.2 %while.19 = (s32[]{:T(128)}, f32[1024,400]{0,1:T(8,128)S(1)}, f32[1024,400]{0,1:T(8,128)S(1)}, f32[16,400]{1,0:T(8,128)S(1)}, s32[4]{0:T(128)S(1)}, /*index=5*/s...) while((s32[]{:T(128)}, f32[1024,400]{0,1:T(8,128)S(1)}, ...), condition=%wide.region_3.4_spmd.clone.clone, body=%wide.region_0.3_spmd.clone.clone.sunk | while | flops 8435658752 | bytes 31468124 | solution.py:150
  119.3 0.6 dynamic_slice.23
  121.1 13.8 %conditional.4 = ((f32[1024,400]{0,1:T(8,128)S(1)}, f32[1024,400]{0,1:T(8,128)S(1)}, f32[16,400]{1,0:T(8,128)S(1)})) conditional(s32[]{:T(128)} %convert_element_type.60, (f32[1024,400]{0,1:T(8,128)S(1)}, f32[1024,400]{0,1:T(8,128)S(1)}, f32[16,400]{1,0:T(8,128)S(1)}) %tuple.60, (s32[]{:T(128)}, s32[4,640]{1,0:T(4,128)S(1)}, s32[1024]{0:T(1024)S(1)}, ...), branch_computations={%region_1.1_spmd, %region_2.0_spmd} | conditional | flops 8435658752 | bytes 31463662 | solution.py:143
  121.1 0.0 copy-start.9
  121.2 2.3 fusion.32
  123.5 0.9 fusion.29
  124.4 1.2 fusion.49
  125.6 0.7 fusion.41
  126.4 0.1 subtract_convert_fusion
  126.5 0.9 multiply_convert_fusion
  127.4 0.6 fusion.43
  128.1 0.7 fusion.67
  128.8 0.2 multiply_add_fusion
  129.0 0.7 convolution_add_fusion
  129.7 2.6 fusion.15
  132.3 2.6 fusion.12
  134.9 0.6 dynamic_slice.23
  136.8 0.6 dynamic_slice.23
  138.6 0.6 dynamic_slice.23
  140.5 0.0 copy-start
  140.5 0.0 copy-start.6
  140.5 1.8 copy.28
  142.3 0.0 all-reduce.3.cloned.1.call-update
  142.4 0.0 all-gather.3.cloned.1.call-start
  142.4 0.5 all-gather.3.cloned.1.call-update
  142.9 122.7 %all-reduce.3.cloned.1.call-done = (f32[1024,400]{0,1:T(8,128)}, f32[64,16,400]{2,1,0:T(8,128)}) async-done(((f32[1024,400]{0,1:T(8,128)}, f32[64,16,400]{2,1,0:T(8,128)}), (f32[1024,400]{0,1:T(8,128)}, f32[64,16,400]{2,1,0:T(8,128)})) %all-reduce.3.cloned.1.call-update) | async-done | bytes 3276816 | tf_op jit(solution)/shard_map/psum | solution.py:153
  265.7 13.3 %all-to-all-start.2 = ((f32[64,16,400]{2,1,0:T(8,128)}), f32[64,16,400]{2,1,0:T(8,128)S(1)}, u32[]{:S(2)}, u32[]{:S(2)}) async-start(f32[64,16,400]{2,1,0:T(8,128)} %get-tuple-element.395), calls=%async_computation.2 | async-start | bytes 4194304 | tf_op jit(solution)/shard_map/all_to_all | solution.py:62
  279.0 1.0 scatter_custom_fusion
  280.0 63.0 %all-to-all-done.2 = f32[64,16,400]{2,1,0:T(8,128)S(1)} async-done(((f32[64,16,400]{2,1,0:T(8,128)}), f32[64,16,400]{2,1,0:T(8,128)S(1)}, u32[]{:S(2)}, u32[]{:S(2)}) %all-to-all-start.2) | async-done | bytes 1638432 | tf_op jit(solution)/shard_map/all_to_all | solution.py:62
  343.0 2.5 fusion.55
  345.5 2.6 copy.30
  348.1 6.8 %all-to-all-start.3 = ((f32[64,16,400]{2,1,0:T(8,128)}), f32[64,16,400]{2,1,0:T(8,128)}, u32[]{:S(2)}, u32[]{:S(2)}) async-start(f32[64,16,400]{2,1,0:T(8,128)} %copy.30), calls=%async_computation.3 | async-start | bytes 4194304 | tf_op jit(solution)/shard_map/all_to_all | solution.py:67
  354.9 0.0 copy-start.13
  354.9 0.0 copy-start.5
  354.9 0.1 multiply_reduce_fusion.1
  355.0 0.5 copy-done.13
  355.6 0.8 copy-done.5
  356.3 1.5 divide_subtract_fusion
  357.8 47.0 %all-to-all-done.3 = f32[64,16,400]{2,1,0:T(8,128)} async-done(((f32[64,16,400]{2,1,0:T(8,128)}), f32[64,16,400]{2,1,0:T(8,128)}, u32[]{:S(2)}, u32[]{:S(2)}) %all-to-all-start.3) | async-done | bytes 1638432 | tf_op jit(solution)/shard_map/all_to_all | solution.py:67
  404.8 3.1 multiply_reduce_fusion
  407.9 0.1 copy.35
  408.0 0.1 copy.32
  408.1 0.1 div.45
  408.2 3.2 fusion.54
  411.4 2.7 copy.34
  414.2 3.9 reduce_sum.38
  418.1 0.1 multiply_reduce_fusion.2
  418.3 0.7 divide_subtract_fusion.1
  (49 shorter events, 0.3 us)
Async XLA Ops:
  9.9 66.7 %copy-start.1 = (f32[1024,400]{1,0:T(8,128)}, f32[1024,400]{1,0:T(8,128)S(1)}, u32[]{:S(2)}) copy-start(f32[1024,400]{1,0:T(8,128)S(1)} %copy.25) | copy-start | bytes 4915204
  9.9 66.7 %copy-start.15 = (s32[64]{0:T(128)S(1)}, s32[64]{0:T(128)}, u32[]{:S(2)}) copy-start(s32[64]{0:T(128)} %param.21) | copy-start | bytes 772
  79.1 8.4 %copy-start.10 = (s32[1,2560]{1,0:T(1,128)S(1)}, s32[1,2560]{1,0:T(1,128)}, u32[]{:S(2)}) copy-start(s32[1,2560]{1,0:T(1,128)} %param.22) | copy-start | bytes 30724
  79.1 8.5 %copy-start.11 = (s32[1,2560]{1,0:T(1,128)S(1)}, s32[1,2560]{1,0:T(1,128)}, u32[]{:S(2)}) copy-start(s32[1,2560]{1,0:T(1,128)} %param.23) | copy-start | bytes 30724
  79.1 8.5 %copy-start.12 = (s32[1,2560]{1,0:T(1,128)S(1)}, s32[1,2560]{1,0:T(1,128)}, u32[]{:S(2)}) copy-start(s32[1,2560]{1,0:T(1,128)} %param.24) | copy-start | bytes 30724
  80.7 7.0 %copy-start.4 = (f32[1024,400]{0,1:T(8,128)S(1)}, f32[1024,400]{0,1:T(8,128)}, u32[]{:S(2)}) copy-start(f32[1024,400]{0,1:T(8,128)} %param.15) | copy-start | bytes 4915204
  80.7 36.9 %all-to-all-start.1 = ((bf16[64,16,400]{2,1,0:T(8,128)(2,1)}), bf16[64,16,400]{2,1,0:T(8,128)(2,1)S(1)}, u32[]{:S(2)}, u32[]{:S(2)}) async-start(bf16[64,16,400]{2,1,0:T(8,128)(2,1)} %copy.27), calls=%async_computation.1 | async-start | bytes 2097152 | tf_op jit(solution)/shard_map/all_to_all | solution.py:67
  87.3 178.4 %all-reduce.3.cloned.1.call-start = ((), (), s32[]{:S(2)}) async-start(), calls=%async_computation.5 | async-start | bytes 7471104 | tf_op jit(solution)/shard_map/psum | solution.py:153
  117.5 1.0 copy-start.8
  118.5 0.8 copy-start.7
  121.1 2.3 copy-start.9
  140.5 1.9 copy-start
  140.5 1.9 copy-start.6
  142.4 271.8 %all-gather.3.cloned.1.call-start = ((), (), s32[]{:S(2)}) async-start(), calls=%async_computation.4 | async-start | bytes 8421376 | tf_op jit(solution)/shard_map/all_gather | solution.py:151
  265.7 77.4 %all-to-all-start.2 = ((f32[64,16,400]{2,1,0:T(8,128)}), f32[64,16,400]{2,1,0:T(8,128)S(1)}, u32[]{:S(2)}, u32[]{:S(2)}) async-start(f32[64,16,400]{2,1,0:T(8,128)} %get-tuple-element.395), calls=%async_computation.2 | async-start | bytes 4194304 | tf_op jit(solution)/shard_map/all_to_all | solution.py:62
  348.1 6.8 %copy-start.3 = (f32[1024,400]{0,1:T(8,128)S(1)}, f32[1024,400]{0,1:T(8,128)}, u32[]{:S(2)}) copy-start(f32[1024,400]{0,1:T(8,128)} %get-tuple-element.394) | copy-start | bytes 4915204
  348.1 56.7 %all-to-all-start.3 = ((f32[64,16,400]{2,1,0:T(8,128)}), f32[64,16,400]{2,1,0:T(8,128)}, u32[]{:S(2)}, u32[]{:S(2)}) async-start(f32[64,16,400]{2,1,0:T(8,128)} %copy.30), calls=%async_computation.3 | async-start | bytes 4194304 | tf_op jit(solution)/shard_map/all_to_all | solution.py:67
  354.9 0.7 copy-start.13
  354.9 1.4 copy-start.5
  357.8 50.4 %copy-start.14 = (f32[1024]{0:T(1024)S(1)}, f32[1024]{0:T(1024)}, u32[]{:S(2)}) copy-start(f32[1024]{0:T(1024)} %param.18) | copy-start | bytes 12292
  357.8 50.4 %copy-start.2 = (f32[1024,400]{1,0:T(8,128)S(1)}, f32[1024,400]{1,0:T(8,128)}, u32[]{:S(2)}) copy-start(f32[1024,400]{1,0:T(8,128)} %copy-done.1) | copy-start | bytes 4915204
  414.2 4.1 copy-start.16
Sparse Core Ops, SparseCore 0:
  142.5 123.1 all-reduce.2
Sparse Core Ops, SparseCore 1:
  147.1 199.7 all-gather.2
